TPU v7x, 128 devices: a whole 4x4x4 slice. The times are simulated.
128 devices in a mesh: mem: 8 (over z, y_lo), lev: 16 (over y_hi, x, core).
Axes of the slice: x: 4, y: 4 (y_hi: 2, y_lo: 2; y = y_hi * 2 + y_lo), z: 4, core: 2. Of those that a mesh axis runs over, the one named last changes fastest.
Arguments:
- control: float32 [8, 64, 200, 400], P('mem', 'lev'), may hold values from -6 to 6
- perturbations: bfloat16 [8, 2, 2, 64, 80000], P('mem', None, None, None, 'lev'), may hold values from -4 to 4
- member_scales: float32 [8], P('mem'), may hold values from 0.05 to 0.2
- vertical_loc: float32 [64, 64], replicated, may hold values from -0.75 to 0.75
- latitude_loc: float32 [200, 200], replicated, may hold values from -0.4375 to 0.4375
- longitude_loc: float32 [400, 400], replicated, may hold values from -0.3125 to 0.3125
- observed_index: int32 [2, 65536], P(None, 'lev'), may hold values from 0 to 639999
- observed_weight: float32 [2, 65536], P(None, 'lev'), may hold values from 0.5 to 8
Outputs:
- hessian_vector: float32 [8, 64, 200, 400], P('mem', 'lev')
All inputs are finite; a program needn't handle non-finite values.
Results may differ from a plain program's by a relative error of at most 0.0003.
Values sent between devices are 32-bit elements; how exact they have to be, the bound alone decides.
No kernel may reach another device: no remote copies, remote signals or barrier semaphores. Data moves between devices by JAX's collectives and lax.ppermute only.
A program may use at most 192 MiB of HBM per device.

v0:
```python
import jax
import jax.numpy as jnp
from jax import lax
from jax.sharding import PartitionSpec as P

HIGH = lax.Precision.HIGHEST


def body(
    control,
    perturbations,
    member_scales,
    vertical_loc,
    latitude_loc,
    longitude_loc,
    observed_index,
    observed_weight,
):
    members, level_count, lat_size, lon_size = control.shape
    rows = jnp.einsum("ab,mlbq->mlaq", latitude_loc, control, precision=HIGH)
    horizontal = jnp.einsum("mlaq,oq->mlao", rows, longitude_loc, precision=HIGH)
    flat_fields = horizontal.reshape(members, level_count, lat_size * lon_size)
    columns = lax.all_to_all(flat_fields, "lev", split_axis=2, concat_axis=1, tiled=True)
    localized = jnp.einsum("lk,mkp->mlp", vertical_loc, columns, precision=HIGH)
    scaled = localized * member_scales[:, None, None]
    slot_count, var_count = (perturbations.shape[1], perturbations.shape[2])
    all_levels, column_width = (perturbations.shape[3], perturbations.shape[4])
    span = all_levels * column_width
    slot_rows = jnp.arange(slot_count, dtype=jnp.int32)[:, None]
    partial_value = perturbations[0].astype(jnp.float32) * scaled[0][None, None]
    obs_grid = jnp.zeros((slot_count, var_count * span), jnp.float32)
    obs_grid = obs_grid.at[slot_rows, observed_index].add(observed_weight)
    obs_grid = obs_grid.reshape(slot_count, var_count, all_levels, column_width)
    increment = lax.psum(partial_value, "mem")
    innovation_adj = obs_grid * increment
    summed = jnp.sum(perturbations[0].astype(jnp.float32) * innovation_adj, axis=(0, 1))
    adjoint_list = [summed * member_scales[0]]
    member_adj = jnp.stack(adjoint_list, axis=0)
    vertical_adj = jnp.einsum("kl,mkp->mlp", vertical_loc, member_adj, precision=HIGH)
    level_fields = lax.all_to_all(vertical_adj, "lev", split_axis=1, concat_axis=2, tiled=True)
    level_fields = level_fields.reshape(members, level_count, lat_size, lon_size)
    back_rows = jnp.einsum("ba,mlbq->mlaq", latitude_loc, level_fields, precision=HIGH)
    return control + jnp.einsum("mlaq,qo->mlao", back_rows, longitude_loc, precision=HIGH)


def solution(mesh):
    placed = (
        P("mem", "lev", None, None),
        P("mem", None, None, None, "lev"),
        P("mem"),
        P(),
        P(),
        P(),
        P(None, "lev"),
        P(None, "lev"),
    )
    return jax.shard_map(
        body, mesh=mesh, in_specs=placed, out_specs=P("mem", "lev", None, None), check_vma=False
    )
```

profile of v0, /device:TPU:1, one launch (start us, length us, event | category | flops | bytes accessed | tf_op | source)
XLA Modules:
  0.0 873.8 jit_solution(12977082701842625879)
XLA Ops:
  6.5 0.0 copy-start
  6.5 4.9 fusion.8
  11.4 0.0 copy-done
  11.4 6.5 fusion.6
  17.9 23.7 %copy.36 = f32[4,200,400]{0,2,1:T(8,128)} copy(f32[4,200,400]{2,1,0:T(8,128)S(1)} %fusion.6) | data formatting | bytes 2560000 | tf_op jit(solution)/shard_map/reshape | solution.py:22
  41.6 0.6 broadcast.25
  42.2 371.8 %reduce.4 = f32[80000,4]{1,0:T(8,128)} reduce(f32[80000,1,4]{2,1,0:T(1,128)} %bitcast.71, f32[]{:T(128)} %broadcast.25), dimensions={1}, to_apply=%bitcast.61.reduce_sub_computation | reduce | bytes 2560004
  414.0 37.7 %reshape.67 = f32[16,1,20000]{2,1,0:T(1,128)} reshape(f32[80000,4]{1,0:T(8,128)} %reduce.4) | data formatting | bytes 2560000
  451.6 8.4 all-to-all-start
  460.1 0.2 all-reduce.2.cloned.1.call-start
  460.9 18.9 %all-to-all-done = f32[16,1,20000]{2,1,0:T(1,128)S(1)} async-done(((f32[16,1,20000]{2,1,0:T(1,128)}), f32[16,1,20000]{2,1,0:T(1,128)S(1)}, u32[]{:S(2)}, u32[]{:S(2)}) %all-to-all-start) | async-done | bytes 1280032 | tf_op jit(solution)/shard_map/all_to_all | solution.py:23
  479.9 3.7 reduce.5
  483.6 85.7 %reshape.68 = f32[80000,1,4]{2,1,0:T(1,128)} reshape(f32[16,20000]{1,0:T(8,128)S(1)} %reduce.5) | data formatting | bytes 2560000
  569.3 21.9 %copy.37 = f32[1,4,16,5000]{3,2,1,0:T(8,128)S(1)} copy(f32[1,4,16,5000]{1,3,2,0:T(8,128)} %bitcast.70) | data formatting | bytes 2560000 | tf_op jit(solution)/shard_map/all_to_all | solution.py:23
  591.2 0.8 copy.27
  592.0 0.0 copy-start.4
  592.0 1.5 reshape.48
  593.6 0.0 copy-start.1
  593.6 0.0 copy-done.4
  593.6 2.8 fusion
  596.3 0.0 copy-done.1
  596.3 3.0 convert_multiply_fusion.1
  599.3 0.0 copy-start.5
  599.3 0.0 copy-start.8
  599.3 0.0 copy-start.7
  599.3 0.0 copy-start.6
  599.3 0.0 all-reduce.2.cloned.1.call-update
  599.4 0.7 copy-done.5
  600.1 0.0 copy-done.8
  600.1 0.1 multiply_reduce_fusion
  600.2 0.0 copy-done.7
  600.2 0.1 and_reduce_fusion
  600.4 0.0 copy-done.6
  600.4 0.6 copy.39
  601.1 45.9 %scatter_custom_fusion = f32[1280000]{0:T(1024)} fusion(s32[8192]{0:T(1024)S(1)} %bitcast.76, f32[8192]{0:T(1024)} %bitcast.77, f32[]{:T(128)} %constant.3.clone.1), kind=kCustom, calls=%fused_computation.7 | custom fusion | flops 8192 | bytes 5120512
  646.9 7.2 reshape.44
  654.2 164.8 %all-reduce.2.cloned.1.call-done = f32[2,2,64,5000]{3,2,1,0:T(8,128)} async-done(((f32[2,2,64,5000]{3,2,1,0:T(8,128)}), f32[2,2,64,5000]{3,2,1,0:T(8,128)}) %all-reduce.2.cloned.1.call-update) | async-done | bytes 5120016 | tf_op jit(solution)/shard_map/psum | solution.py:34
  819.0 5.5 fusion.1
  824.5 1.4 convolution_bitcast_fusion
  825.9 1.3 copy.28
  827.2 27.5 %all_to_all.30 = f32[1,64,5000]{2,0,1:T(1,128)S(1)} all-to-all(f32[1,64,5000]{2,0,1:T(1,128)S(1)} %copy.28), channel_id=1, replica_groups=mesh['mem'=8,'lev'=16] {'lev'}, dimensions={1} | all-to-all | bytes 2560000 | tf_op jit(solution)/shard_map/all_to_all | solution.py:40
  854.7 1.8 copy.41
  856.6 0.0 copy-start.3
  856.6 2.0 reshape.49
  858.5 0.0 copy-done.3
  858.6 0.0 copy-start.2
  858.6 3.3 fusion.16
  861.9 0.0 copy-done.2
  861.9 4.8 bitcast_add_fusion
  (4 shorter events, 0.1 us)
Async XLA Ops:
  6.5 4.9 copy-start
  451.6 28.2 %all-to-all-start = ((f32[16,1,20000]{2,1,0:T(1,128)}), f32[16,1,20000]{2,1,0:T(1,128)S(1)}, u32[]{:S(2)}, u32[]{:S(2)}) async-start(f32[16,1,20000]{2,1,0:T(1,128)} %reshape.67), calls=%async_computation | async-start | bytes 2572288 | tf_op jit(solution)/shard_map/all_to_all | solution.py:23
  460.1 358.9 %all-reduce.2.cloned.1.call-start = ((), (), s32[]{:S(2)}) async-start(), calls=%async_computation.2 | async-start | bytes 10485760 | tf_op jit(solution)/shard_map/psum | solution.py:34
  592.0 1.5 copy-start.4
  593.6 2.8 copy-start.1
  599.3 0.8 copy-start.5
  599.3 0.8 copy-start.8
  599.3 0.9 copy-start.7
  599.3 1.1 copy-start.6
  856.6 2.0 copy-start.3
  858.6 3.3 copy-start.2
Sparse Core Ops, SparseCore 0:
  599.5 219.4 all-reduce.1
where the time goes:
time: 881 us; the launch traced here: 874 us
  other arithmetic  430 us (49%)
  local copies, waits for them, and re-layouts  186 us (21%)
  waiting for transfers between devices  184 us (21%)
  blocking collectives  27.5 us (3%)
  matrix products  23.6 us (3%)
  between operations  14.5 us (2%)
    unnamed x5, other arithmetic  418 us
    psum x1, waiting for transfers between devices, body(): increment = lax.psum(partial_value, 'mem')  165 us
    unnamed x23, local copies, waits for them, and re-layouts  125 us
    all_to_all x1, blocking collectives, body(): lax.all_to_all(vertical_adj, 'lev', split_axis=1, concat_axis=2, tiled=True)  27.5 us
    reshape x1, local copies, waits for them, and re-layouts, body(): flat_fields = horizontal.reshape(members, level_count, lat_size * lon_size)  23.7 us
    all_to_all x2, local copies, waits for them, and re-layouts, body(): lax.all_to_all(flat_fields, 'lev', split_axis=2, concat_axis=1, tiled=True)  22.7 us
    all_to_all x1, waiting for transfers between devices, body(): lax.all_to_all(flat_fields, 'lev', split_axis=2, concat_axis=1, tiled=True)  18.9 us
  transfers between devices with their start and end apart: 2, of which 2 were waited for; matrix products, arithmetic and copies ran while one was open for 6% of the time, Pallas kernels for 0%

commit v1 on v0

--- a/solution.py
+++ b/solution.py
@@ -20,7 +20,12 @@
     rows = jnp.einsum("ab,mlbq->mlaq", latitude_loc, control, precision=HIGH)
     horizontal = jnp.einsum("mlaq,oq->mlao", rows, longitude_loc, precision=HIGH)
     flat_fields = horizontal.reshape(members, level_count, lat_size * lon_size)
-    columns = lax.all_to_all(flat_fields, "lev", split_axis=2, concat_axis=1, tiled=True)
+    columns = jnp.concatenate(
+        lax.all_to_all(
+            jnp.stack(jnp.split(flat_fields, lax.axis_size("lev"), axis=2)), "lev", 0, 0
+        ),
+        axis=1,
+    )
     localized = jnp.einsum("lk,mkp->mlp", vertical_loc, columns, precision=HIGH)
     scaled = localized * member_scales[:, None, None]
     slot_count, var_count = (perturbations.shape[1], perturbations.shape[2])

time: 881 us -> 350 us (0.40)
  other arithmetic: 430 us -> 54.6 us
  local copies, waits for them, and re-layouts: 186 us -> 36.6 us
    unnamed x5 -> x4, other arithmetic: 418 us -> 46.1 us
    unnamed x23 -> x37, local copies, waits for them, and re-layouts: 125 us -> 19.7 us
    all_to_all x2 -> x0, local copies, waits for them, and re-layouts: 22.7 us -> none  [body(): lax.all_to_all(flat_fields, 'lev', split_axis=2, concat_axis=1, tiled=True)]
    reshape x1, local copies, waits for them, and re-layouts: 23.7 us -> 2.43 us  [body(): flat_fields = horizontal.reshape(members, level_count, lat_size * lon_size)]
  transfers between devices with their start and end apart: 2 -> 2, of which waited for: 2 -> 2; matrix products, arithmetic and copies ran while one was open for 6% -> 15% of each run, Pallas kernels for 0% -> 0%
where the time goes in v1:
time: 350 us; the launch traced here: 349 us
  waiting for transfers between devices  184 us (53%)
  other arithmetic  54.6 us (16%)
  local copies, waits for them, and re-layouts  36.6 us (10%)
  blocking collectives  27.3 us (8%)
  matrix products  23.6 us (7%)
  between operations  14.2 us (4%)
  starting transfers between devices  8.65 us (2%)
    psum x1, waiting for transfers between devices, body(): increment = lax.psum(partial_value, 'mem')  165 us
    unnamed x4, other arithmetic  46.1 us
    all_to_all x1, blocking collectives, body(): lax.all_to_all(vertical_adj, 'lev', split_axis=1, concat_axis=2, tiled=True)  27.3 us
    unnamed x37, local copies, waits for them, and re-layouts  19.7 us
    all_to_all x1, waiting for transfers between devices, body(): lax.all_to_all(jnp.stack(jnp.split(flat_fields, lax.axis_size('lev'), axi...  19.2 us
    all_to_all x1, starting transfers between devices, body(): lax.all_to_all(jnp.stack(jnp.split(flat_fields, lax.axis_size('lev'), axi...  8.43 us
    reshape x1, local copies, waits for them, and re-layouts, body(): obs_grid = obs_grid.reshape(slot_count, var_count, all_levels, column_width)  7.09 us
  transfers between devices with their start and end apart: 2, of which 2 were waited for; matrix products, arithmetic and copies ran while one was open for 15% of the time, Pallas kernels for 0%

profile of v1, /device:TPU:1, one launch (start us, length us, event | category | flops | bytes accessed | tf_op | source)
XLA Modules:
  0.0 349.2 jit_solution(3177430189921122589)
XLA Ops:
  6.5 0.0 copy-start
  6.5 4.9 %fusion.8 = f32[4,400,200]{2,1,0:T(8,128)S(1)} fusion(f32[1,4,200,400]{3,2,1,0:T(8,128)} %param.8, f32[200,200]{1,0:T(8,128)} %param.12), kind=kOutput, calls=%fused_computation.14 | convolution fusion | flops 768000000 | bytes 2720000 | tf_op jit(solution)/shard_map/ab,mlbq->mlaq/dot_general | solution.py:20
  11.4 0.0 copy-done
  11.4 6.5 %fusion.6 = f32[4,200,400]{2,1,0:T(8,128)S(1)} fusion(f32[4,400,200]{2,1,0:T(8,128)S(1)} %fusion.8, f32[400,400]{1,0:T(8,128)S(1)} %copy-done), kind=kOutput, calls=%fused_computation.11 | convolution fusion | flops 1536000000 | bytes 3200000 | tf_op jit(solution)/shard_map/mlaq,oq->mlao/dot_general | solution.py:21
  17.9 2.4 reshape.48
  20.3 0.0 copy-start.3
  20.3 1.6 fusion.34
  22.0 1.6 fusion.33
  23.6 1.6 fusion.32
  25.2 1.6 fusion.31
  26.9 1.6 fusion.30
  28.5 1.6 fusion.29
  30.1 1.6 fusion.28
  31.8 1.6 fusion.27
  33.4 0.0 copy-done.3
  33.4 0.7 fusion.26
  34.1 0.7 fusion.25
  34.9 0.7 fusion.24
  35.6 0.7 fusion.23
  36.4 0.7 fusion.22
  37.1 0.7 fusion.21
  37.9 0.7 fusion.20
  38.6 0.7 fusion.19
  39.4 8.4 %all-to-all-start = ((f32[16,1,4,5000]{3,2,1,0:T(4,128)}), f32[16,1,4,5000]{3,2,1,0:T(4,128)S(1)}, u32[]{:S(2)}, u32[]{:S(2)}) async-start(f32[16,1,4,5000]{3,2,1,0:T(4,128)} %fusion.19), calls=%async_computation | async-start | bytes 2621440 | tf_op jit(solution)/shard_map/all_to_all | solution.py:24
  47.8 0.2 all-reduce.2.cloned.1.call-start
  48.7 0.0 copy-start.5
  48.7 19.2 %all-to-all-done = f32[16,1,4,5000]{3,2,1,0:T(4,128)S(1)} async-done(((f32[16,1,4,5000]{3,2,1,0:T(4,128)}), f32[16,1,4,5000]{3,2,1,0:T(4,128)S(1)}, u32[]{:S(2)}, u32[]{:S(2)}) %all-to-all-start) | async-done | bytes 1280032 | tf_op jit(solution)/shard_map/all_to_all | solution.py:24
  67.9 1.5 reshape.49
  69.4 0.0 copy-done.5
  69.4 0.0 copy-start.1
  69.4 2.8 fusion
  72.2 0.0 copy-done.1
  72.2 3.0 convert_multiply_fusion.1
  75.1 0.0 copy-start.6
  75.1 0.0 copy-start.8
  75.1 0.0 copy-start.9
  75.1 0.0 copy-start.7
  75.1 0.0 all-reduce.2.cloned.1.call-update
  75.2 0.7 copy-done.6
  75.9 0.0 copy-done.8
  75.9 0.1 multiply_reduce_fusion
  76.0 0.0 copy-done.9
  76.0 0.1 and_reduce_fusion
  76.2 0.0 copy-done.7
  76.2 0.6 copy.28
  76.9 45.9 %scatter_custom_fusion = f32[1280000]{0:T(1024)} fusion(s32[8192]{0:T(1024)S(1)} %bitcast.132, f32[8192]{0:T(1024)} %bitcast.133, f32[]{:T(128)} %constant.3.clone.1), kind=kCustom, calls=%fused_computation.7 | custom fusion | flops 8192 | bytes 5120512
  122.7 7.1 %reshape.45 = f32[2,2,64,5000]{3,2,1,0:T(8,128)} reshape(f32[1280000]{0:T(1024)} %scatter_custom_fusion) | data formatting | bytes 10240000 | tf_op jit(solution)/shard_map/reshape | solution.py:38
  129.8 165.0 %all-reduce.2.cloned.1.call-done = f32[2,2,64,5000]{3,2,1,0:T(8,128)} async-done(((f32[2,2,64,5000]{3,2,1,0:T(8,128)}), f32[2,2,64,5000]{3,2,1,0:T(8,128)}) %all-reduce.2.cloned.1.call-update) | async-done | bytes 5120016 | tf_op jit(solution)/shard_map/psum | solution.py:39
  294.8 5.5 %fusion.1 = f32[64,5000]{1,0:T(8,128)S(1)} fusion(f32[2,2,64,5000]{3,2,1,0:T(8,128)} %reshape.45, f32[2,2,64,5000]{3,2,1,0:T(8,128)} %all-reduce.2.cloned.1.call-done, bf16[1,2,2,64,5000]{4,3,2,1,0:T(8,128)(2,1)S(1)} %copy-done.1), kind=kLoop, calls=%fused_computation.6 | loop fusion | flops 4800000 | bytes 14080000 | tf_op jit(solution)/shard_map/reduce_sum | solution.py:41
  300.3 1.4 convolution_bitcast_fusion
  301.7 1.3 copy.19
  303.1 27.3 %all_to_all.20 = f32[1,64,5000]{2,0,1:T(1,128)S(1)} all-to-all(f32[1,64,5000]{2,0,1:T(1,128)S(1)} %copy.19), channel_id=1, replica_groups=mesh['mem'=8,'lev'=16] {'lev'}, dimensions={1} | all-to-all | bytes 2560000 | tf_op jit(solution)/shard_map/all_to_all | solution.py:45
  330.4 1.8 copy.30
  332.2 0.0 copy-start.4
  332.2 2.0 reshape.50
  334.2 0.0 copy-done.4
  334.2 0.0 copy-start.2
  334.2 3.3 fusion.16
  337.5 0.0 copy-done.2
  337.5 4.8 %bitcast_add_fusion = f32[1,4,200,400]{3,2,1,0:T(8,128)} fusion(f32[1,4,200,400]{3,2,1,0:T(8,128)S(1)} %copy-done.2, f32[4,400,200]{2,1,0:T(8,128)S(1)} %fusion.16, f32[400,400]{1,0:T(8,128)S(1)} %copy-done), kind=kOutput, calls=%fused_computation.13 | convolution fusion | flops 1536320000 | bytes 4480000 | tf_op jit(solution)/shard_map/mlaq,qo->mlao/dot_general | solution.py:48
  (4 shorter events, 0.1 us)
Async XLA Ops:
  6.5 4.9 %copy-start = (f32[400,400]{1,0:T(8,128)S(1)}, f32[400,400]{1,0:T(8,128)}, u32[]{:S(2)}) copy-start(f32[400,400]{1,0:T(8,128)} %param.13) | copy-start | bytes 1920004
  20.3 13.1 %copy-start.3 = (f32[1,4,80000]{2,1,0:T(4,128)S(1)}, f32[1,4,80000]{2,1,0:T(4,128)}, u32[]{:S(2)}) copy-start(f32[1,4,80000]{2,1,0:T(4,128)} %reshape.48) | copy-start | bytes 3840004
  39.4 28.5 %all-to-all-start = ((f32[16,1,4,5000]{3,2,1,0:T(4,128)}), f32[16,1,4,5000]{3,2,1,0:T(4,128)S(1)}, u32[]{:S(2)}, u32[]{:S(2)}) async-start(f32[16,1,4,5000]{3,2,1,0:T(4,128)} %fusion.19), calls=%async_computation | async-start | bytes 2621440 | tf_op jit(solution)/shard_map/all_to_all | solution.py:24
  47.8 247.1 %all-reduce.2.cloned.1.call-start = ((), (), s32[]{:S(2)}) async-start(), calls=%async_computation.2 | async-start | bytes 10485760 | tf_op jit(solution)/shard_map/psum | solution.py:39
  48.7 20.7 %copy-start.5 = (f32[64,64]{1,0:T(8,128)S(1)}, f32[64,64]{1,0:T(8,128)}, u32[]{:S(2)}) copy-start(f32[64,64]{1,0:T(8,128)} %param.11) | copy-start | bytes 49156
  69.4 2.8 copy-start.1
  75.1 0.8 copy-start.6
  75.1 0.8 copy-start.8
  75.1 0.9 copy-start.9
  75.1 1.1 copy-start.7
  332.2 2.0 copy-start.4
  334.2 3.3 copy-start.2
Sparse Core Ops, SparseCore 0:
  75.3 219.5 all-reduce.1

commit v2 on v0

--- a/solution.py
+++ b/solution.py
@@ -31,7 +31,7 @@
     obs_grid = jnp.zeros((slot_count, var_count * span), jnp.float32)
     obs_grid = obs_grid.at[slot_rows, observed_index].add(observed_weight)
     obs_grid = obs_grid.reshape(slot_count, var_count, all_levels, column_width)
-    increment = lax.psum(partial_value, "mem")
+    increment = jnp.sum(lax.all_gather(partial_value, "mem"), axis=0)
     innovation_adj = obs_grid * increment
     summed = jnp.sum(perturbations[0].astype(jnp.float32) * innovation_adj, axis=(0, 1))
     adjoint_list = [summed * member_scales[0]]

time: 881 us -> 1470 us (1.67)
  waiting for transfers between devices: 184 us -> 759 us
  other arithmetic: 430 us -> 448 us
    all_gather x0 -> x1, waiting for transfers between devices: none -> 740 us  [body(): increment = jnp.sum(lax.all_gather(partial_value, 'mem'), axis=0)]
    psum x1 -> x0, waiting for transfers between devices: 165 us -> none  [body(): increment = lax.psum(partial_value, 'mem')]
    reduce_sum x0 -> x1, other arithmetic: none -> 18.1 us  [body(): increment = jnp.sum(lax.all_gather(partial_value, 'mem'), axis=0)]
  transfers between devices with their start and end apart: 2 -> 2, of which waited for: 2 -> 2; matrix products, arithmetic and copies ran while one was open for 6% -> 4% of each run, Pallas kernels for 0% -> 0%
where the time goes in v2:
time: 1470 us
  waiting for transfers between devices  759 us (52%)
  other arithmetic  448 us (30%)
  local copies, waits for them, and re-layouts  186 us (13%)
  blocking collectives  27.2 us (2%)
  matrix products  23.6 us (2%)
    all_gather x1, waiting for transfers between devices, body(): increment = jnp.sum(lax.all_gather(partial_value, 'mem'), axis=0)  740 us
    unnamed x5, other arithmetic  418 us
    unnamed x23, local copies, waits for them, and re-layouts  125 us
  transfers between devices with their start and end apart: 2, of which 2 were waited for; matrix products, arithmetic and copies ran while one was open for 4% of the time, Pallas kernels for 0%

profile of v2, /device:TPU:1, one launch (start us, length us, event | category | flops | bytes accessed | tf_op | source)
XLA Modules:
  0.0 1467.1 jit_solution(9299228699560873250)
XLA Ops:
  6.5 0.0 copy-start
  6.5 4.9 fusion.9
  11.4 0.0 copy-done
  11.4 6.5 fusion.7
  17.9 23.7 %copy.36 = f32[4,200,400]{0,2,1:T(8,128)} copy(f32[4,200,400]{2,1,0:T(8,128)S(1)} %fusion.7) | data formatting | bytes 2560000 | tf_op jit(solution)/shard_map/reshape | solution.py:22
  41.6 0.6 broadcast.26
  42.2 371.8 %reduce.4 = f32[80000,4]{1,0:T(8,128)} reduce(f32[80000,1,4]{2,1,0:T(1,128)} %bitcast.73, f32[]{:T(128)} %broadcast.26), dimensions={1}, to_apply=%bitcast.63.reduce_sub_computation | reduce | bytes 2560004
  414.0 37.7 %reshape.67 = f32[16,1,20000]{2,1,0:T(1,128)} reshape(f32[80000,4]{1,0:T(8,128)} %reduce.4) | data formatting | bytes 2560000
  451.6 8.4 all-to-all-start
  460.1 0.2 all-gather.2.cloned.1.call-start
  460.9 18.9 %all-to-all-done = f32[16,1,20000]{2,1,0:T(1,128)S(1)} async-done(((f32[16,1,20000]{2,1,0:T(1,128)}), f32[16,1,20000]{2,1,0:T(1,128)S(1)}, u32[]{:S(2)}, u32[]{:S(2)}) %all-to-all-start) | async-done | bytes 1280032 | tf_op jit(solution)/shard_map/all_to_all | solution.py:23
  479.9 3.7 reduce.5
  483.6 85.7 %reshape.68 = f32[80000,1,4]{2,1,0:T(1,128)} reshape(f32[16,20000]{1,0:T(8,128)S(1)} %reduce.5) | data formatting | bytes 2560000
  569.3 21.9 %copy.37 = f32[1,4,16,5000]{3,2,1,0:T(8,128)S(1)} copy(f32[1,4,16,5000]{1,3,2,0:T(8,128)} %bitcast.72) | data formatting | bytes 2560000 | tf_op jit(solution)/shard_map/all_to_all | solution.py:23
  591.2 0.8 copy.27
  592.0 0.0 copy-start.4
  592.0 1.5 reshape.48
  593.6 0.0 copy-start.1
  593.6 0.0 copy-done.4
  593.6 2.8 fusion
  596.3 0.0 copy-done.1
  596.3 2.9 convert_multiply_fusion
  599.2 0.0 copy-start.5
  599.2 0.0 copy-start.8
  599.2 0.0 copy-start.7
  599.2 0.0 copy-start.6
  599.2 0.0 all-gather.2.cloned.1.call-update
  599.2 0.7 copy-done.5
  600.0 0.0 copy-done.8
  600.0 0.1 multiply_reduce_fusion
  600.1 0.0 copy-done.7
  600.1 0.1 and_reduce_fusion
  600.3 0.0 copy-done.6
  600.3 0.6 copy.39
  601.0 45.9 %scatter_custom_fusion = f32[1280000]{0:T(1024)} fusion(s32[8192]{0:T(1024)S(1)} %bitcast.78, f32[8192]{0:T(1024)} %bitcast.79, f32[]{:T(128)} %constant.3.clone.1), kind=kCustom, calls=%fused_computation.8 | custom fusion | flops 8192 | bytes 5120512
  646.9 7.3 reshape.44
  654.2 740.3 %all-gather.2.cloned.1.call-done = f32[8,2,2,64,5000]{4,3,2,1,0:T(8,128)} async-done(((f32[1,2,2,64,5000]{4,3,2,1,0:T(8,128)}), f32[8,2,2,64,5000]{4,3,2,1,0:T(8,128)}) %all-gather.2.cloned.1.call-update) | async-done | bytes 40960016 | tf_op jit(solution)/shard_map/all_gather | solution.py:34
  1394.5 18.1 %reduce_sum.18 = f32[2,2,64,5000]{3,2,1,0:T(8,128)} reduce(f32[8,2,2,64,5000]{4,3,2,1,0:T(8,128)} %all-gather.2.cloned.1.call-done, f32[]{:T(128)} %constant.3.clone.1), dimensions={0}, to_apply=%region_1.0 | reduce | flops 8960000 | bytes 46080004 | tf_op jit(solution)/shard_map/reduce_sum | solution.py:34
  1412.7 5.5 fusion.2
  1418.2 1.4 convolution_bitcast_fusion
  1419.5 1.3 copy.28
  1420.9 27.2 %all_to_all.30 = f32[1,64,5000]{2,0,1:T(1,128)S(1)} all-to-all(f32[1,64,5000]{2,0,1:T(1,128)S(1)} %copy.28), channel_id=1, replica_groups=mesh['mem'=8,'lev'=16] {'lev'}, dimensions={1} | all-to-all | bytes 2560000 | tf_op jit(solution)/shard_map/all_to_all | solution.py:40
  1448.1 1.8 copy.41
  1449.9 0.0 copy-start.3
  1449.9 2.0 reshape.49
  1451.9 0.0 copy-done.3
  1451.9 0.0 copy-start.2
  1451.9 3.3 fusion.17
  1455.2 0.0 copy-done.2
  1455.2 4.8 bitcast_add_fusion
  (4 shorter events, 0.1 us)
Async XLA Ops:
  6.5 4.9 copy-start
  451.6 28.2 %all-to-all-start = ((f32[16,1,20000]{2,1,0:T(1,128)}), f32[16,1,20000]{2,1,0:T(1,128)S(1)}, u32[]{:S(2)}, u32[]{:S(2)}) async-start(f32[16,1,20000]{2,1,0:T(1,128)} %reshape.67), calls=%async_computation | async-start | bytes 2572288 | tf_op jit(solution)/shard_map/all_to_all | solution.py:23
  460.1 934.5 %all-gather.2.cloned.1.call-start = ((), (), s32[]{:S(2)}) async-start(), calls=%async_computation.2 | async-start | bytes 47185920 | tf_op jit(solution)/shard_map/all_gather | solution.py:34
  592.0 1.5 copy-start.4
  593.6 2.8 copy-start.1
  599.2 0.8 copy-start.5
  599.2 0.8 copy-start.8
  599.2 0.9 copy-start.7
  599.2 1.1 copy-start.6
  1449.9 2.0 copy-start.3
  1451.9 3.3 copy-start.2
Sparse Core Ops, SparseCore 0:
  599.4 795.1 all-gather.1
